TPU v7x, 32 devices: a whole 2x2x4 slice. The times are simulated.
32 devices in a mesh: tm: 32 (over z, y, x, core).
Axes of the slice: x: 2, y: 2, z: 4, core: 2. Of those that a mesh axis runs over, the one named last changes fastest.
Arguments:
- wrapped: float32 [4096, 3, 512], P('tm'), may hold values from 0 to 1, as said below
- crossings: int32 [4096, 3, 512], P('tm'), may hold values from -1 to 1, as said below
- box_size: float32 [3], replicated, may hold values from 4 to 12
Outputs:
- msd: float32 [512, 128], P('tm')
Inputs may be any that keep to these rules, and one draw needn't show every extreme that they name: `wrapped`: scaled coordinates within the unit cell. per-frame crossings, one of -1, 0, 1; most entries are 0.
All inputs are finite; a program needn't handle non-finite values.
Results may differ from a plain program's by a relative error of at most 0.0003.
Values sent between devices are 32-bit elements; how exact they have to be, the bound alone decides.
A program may use at most 64 MiB of HBM per device.

v0:
```python
import functools

import jax
import jax.numpy as jnp
from jax import lax
from jax.experimental import pallas as pl
from jax.experimental.pallas import tpu as pltpu
from jax.sharding import PartitionSpec as P

LAGS = 128
LANES = 128
SUB = 8
MESH = pl.DeviceIdType.MESH


def kernel(n, wrapped, crossings, box, out, wbuf, xbuf, sbuf, hbuf, mean_buf, delta_buf,
           ext, sq, lagbuf, tbuf, rbuf, load_sem, halo_send, halo_recv, part_send, part_recv):
    dims, depth = wbuf.shape[0], wbuf.shape[1]
    frames = SUB * depth
    groups = sbuf.shape[0]
    per_owner = out.shape[0]
    owners = LANES // per_owner
    me = lax.axis_index("tm")
    is_last = me == n - 1
    prev = lax.rem(me + n - 1, n)
    nxt = lax.rem(me + 1, n)

    def load(i, which):
        c, s = i // SUB, lax.rem(i, SUB)
        src, dst = ((wrapped, wbuf), (crossings, xbuf))[which]
        return pltpu.make_async_copy(src.at[s, :, c, :], dst.at[c, :, s, :], load_sem.at[which, i])

    @pl.loop(0, dims * SUB)
    def _(i):
        load(i, 0).start()
        load(i, 1).start()

    barrier = pltpu.get_barrier_semaphore()

    @pl.loop(1, n)
    def _(o):
        pl.semaphore_signal(barrier, inc=1, device_id=(lax.rem(me + o, n),), device_id_type=MESH)

    @pl.loop(0, dims * SUB)
    def _(i):
        load(i, 0).wait()
        load(i, 1).wait()

    sub_ids = lax.broadcasted_iota(jnp.int32, (SUB, LANES), 0)

    def halo(i):
        return pltpu.make_async_remote_copy(
            src_ref=sbuf.at[i // dims, lax.rem(i, dims)],
            dst_ref=hbuf.at[i // dims, lax.rem(i, dims)],
            send_sem=halo_send.at[i], recv_sem=halo_recv.at[i],
            device_id=(prev,), device_id_type=MESH)

    def first_group(device):
        return device * groups // n + 1

    def prepare(step):
        g = lax.rem(step // dims + first_group(prev), groups)
        c = lax.rem(step, dims)
        lanes = pl.ds(pl.multiple_of(g * LANES, LANES), LANES)
        box_len = box[c]
        counts = [xbuf[c, 0, :, lanes].astype(jnp.float32)]
        for r in range(1, depth):
            counts.append(counts[-1] + xbuf[c, r, :, lanes].astype(jnp.float32))
        incl = counts[-1]
        for shift in (1, 2, 4):
            incl = incl + jnp.where(sub_ids >= shift, pltpu.roll(incl, shift, 0), 0.0)
        total = jnp.broadcast_to(incl[SUB - 1:SUB, :], (SUB, LANES))
        before = incl - counts[-1]
        tot_pos = jnp.zeros((SUB, LANES), jnp.float32)
        for r in range(depth):
            pos = (wbuf[c, r, :, lanes] + (counts[r] + before)) * box_len
            sbuf[g, c, r] = pos
            tot_pos = tot_pos + pos
        mean = jnp.broadcast_to(jnp.sum(tot_pos, axis=0, keepdims=True), (SUB, LANES)) * (1.0 / frames)
        mean_buf[g, c] = mean
        delta_buf[g, c] = total * box_len - mean
        return g * dims + c

    pl.semaphore_wait(barrier, n - 1)

    @pl.loop(0, groups * dims)
    def _(step):
        i = prepare(step)

        @pl.when(me > 0)
        def _():
            halo(i).start()

    end_row = jnp.where(is_last, SUB, 4 * SUB)

    def part(g, d):
        owner = g * owners + d
        return owner, pltpu.make_async_remote_copy(
            src_ref=tbuf.at[owner], dst_ref=rbuf.at[me],
            send_sem=part_send.at[owner], recv_sem=part_recv.at[me],
            device_id=(owner,), device_id_type=MESH)

    @pl.loop(0, groups)
    def _(gi):
        g = lax.rem(gi + first_group(me), groups)

        @pl.loop(0, LAGS)
        def _(k):
            lagbuf[pl.ds(pl.multiple_of(k * SUB, SUB), SUB), :] = jnp.zeros((SUB, LANES), jnp.float32)

        sq[...] = jnp.zeros_like(sq)

        @pl.loop(0, dims)
        def _(c):
            mean, delta = mean_buf[g, c], delta_buf[g, c]
            for r in range(depth):
                own = sbuf[g, c, r] - mean
                ext[r, 0:SUB, :] = own
                sq[r, 0:SUB, :] = sq[r, 0:SUB, :] + own * own

            @pl.when(is_last)
            def _():
                for r in range(depth):
                    ext[r, SUB:2 * SUB, :] = jnp.zeros((SUB, LANES), jnp.float32)

            @pl.when(jnp.logical_not(is_last))
            def _():
                halo(g * dims + c).wait_recv()
                for r in range(depth):
                    far = hbuf[g, c, r] + delta
                    ext[r, SUB:2 * SUB, :] = far
                    sq[r, SUB:2 * SUB, :] = sq[r, SUB:2 * SUB, :] + far * far

            @pl.loop(0, LAGS // depth)
            def _(q):
                near = [ext[r, 0:SUB, :] * -2.0 for r in range(depth)]
                rows = [pl.ds(pl.multiple_of((q * depth + j) * SUB, SUB), SUB) for j in range(depth)]
                acc = [None] * depth
                for m in range(2 * depth - 1):
                    far = ext[m % depth, pl.ds(q + m // depth, SUB), :]
                    for r in range(max(0, m - depth + 1), min(depth - 1, m) + 1):
                        j = m - r
                        term = far * near[r]
                        acc[j] = term if acc[j] is None else acc[j] + term
                        if r == depth - 1:
                            lagbuf[rows[j], :] = lagbuf[rows[j], :] + acc[j]

        own_total = sq[0, 0:SUB, :]
        for r in range(1, depth):
            own_total = own_total + sq[r, 0:SUB, :]

        @pl.loop(0, LAGS // depth)
        def _(q):
            row = sub_ids + q
            near_sum = own_total
            far_sum = sq[0, pl.ds(q, SUB), :]
            for r in range(1, depth):
                far_sum = far_sum + sq[r, pl.ds(q, SUB), :]
            for j in range(depth):
                base = jnp.where(row >= end_row, 0.0, jnp.where(row == end_row - 1, near_sum, own_total))
                rows = pl.ds(pl.multiple_of((q * depth + j) * SUB, SUB), SUB)
                lagbuf[rows, :] = lagbuf[rows, :] + (base + far_sum)
                if j < depth - 1:
                    near_sum = near_sum - sq[depth - 1 - j, 0:SUB, :]
                    far_sum = far_sum + (sq[j, pl.ds(q + 1, SUB), :] - sq[j, pl.ds(q, SUB), :])

        blocks = []
        for kb in range(LAGS // SUB):
            val = lagbuf[pl.ds(kb * SUB * SUB, SUB, stride=SUB), :]
            for s in range(1, SUB):
                val = val + lagbuf[pl.ds(kb * SUB * SUB + s, SUB, stride=SUB), :]
            blocks.append(val)
        by_atom = jnp.concatenate(blocks, axis=0).T
        for d in range(owners):
            tbuf[g * owners + d] = by_atom[d * per_owner:(d + 1) * per_owner, :]

        @pl.loop(0, owners)
        def _(d):
            owner, copy = part(g, d)

            @pl.when(owner != me)
            def _():
                copy.start()

    out[...] = tbuf[me]

    @pl.loop(1, n)
    def _(o):
        src = lax.rem(me + o, n)
        pltpu.make_async_remote_copy(
            src_ref=tbuf.at[src], dst_ref=rbuf.at[src],
            send_sem=part_send.at[src], recv_sem=part_recv.at[src],
            device_id=(src,), device_id_type=MESH).wait()
        out[...] = out[...] + rbuf[src]

    lag_ids = lax.broadcasted_iota(jnp.int32, (per_owner, LAGS), 1)
    out[...] = out[...] / (n * frames - lag_ids).astype(jnp.float32)

    @pl.when(me > 0)
    def _():
        @pl.loop(0, groups * dims)
        def _(i):
            halo(i).wait_send()


def on_device(n, wrapped, crossings, box_size):
    frames, dims, atoms = wrapped.shape
    depth, groups = frames // SUB, atoms // LANES
    per_owner = atoms // n
    assert frames == LAGS and atoms % LANES == 0 and LANES % per_owner == 0
    split = (SUB, depth, dims, atoms)
    any_spec = pl.BlockSpec(memory_space=pl.ANY)
    f32 = jnp.float32
    return pl.pallas_call(
        functools.partial(kernel, n),
        out_shape=jax.ShapeDtypeStruct((per_owner, LAGS), f32),
        in_specs=[any_spec, any_spec, pl.BlockSpec(memory_space=pltpu.SMEM)],
        out_specs=pl.BlockSpec(memory_space=pltpu.VMEM),
        scratch_shapes=[
            pltpu.VMEM((dims, depth, SUB, atoms), f32),
            pltpu.VMEM((dims, depth, SUB, atoms), jnp.int32),
            pltpu.VMEM((groups, dims, depth, SUB, LANES), f32),
            pltpu.VMEM((groups, dims, depth, SUB, LANES), f32),
            pltpu.VMEM((groups, dims, SUB, LANES), f32),
            pltpu.VMEM((groups, dims, SUB, LANES), f32),
            pltpu.VMEM((depth, 2 * SUB, LANES), f32),
            pltpu.VMEM((depth, 2 * SUB, LANES), f32),
            pltpu.VMEM((LAGS * SUB, LANES), f32),
            pltpu.VMEM((n, per_owner, LAGS), f32),
            pltpu.VMEM((n, per_owner, LAGS), f32),
            pltpu.SemaphoreType.DMA((2, dims * SUB)),
            pltpu.SemaphoreType.DMA((groups * dims,)),
            pltpu.SemaphoreType.DMA((groups * dims,)),
            pltpu.SemaphoreType.DMA((n,)),
            pltpu.SemaphoreType.DMA((n,)),
        ],
        compiler_params=pltpu.CompilerParams(collective_id=0, has_side_effects=True),
    )(wrapped.reshape(split), crossings.reshape(split), box_size)


def solution(mesh):
    in_specs = (P("tm", None, None), P("tm", None, None), P())
    out_specs = P("tm", None)
    return jax.shard_map(
        functools.partial(on_device, mesh.shape["tm"]), mesh=mesh,
        in_specs=in_specs, out_specs=out_specs, check_vma=False)
```

profile of v0, /device:TPU:0, one launch (start us, length us, event | category | flops | bytes accessed | tf_op | source)
XLA Modules:
  0.0 34.6 jit_solution(8834830046343314562)
XLA Ops:
  0.0 0.0 copy-start
  0.0 2.7 %copy.4 = f32[128,3,512]{2,1,0:T(4,128)} copy(f32[128,3,512]{2,0,1:T(8,128)} %param.3) | data formatting | bytes 1572864 | tf_op args[0]
  2.7 0.0 copy-done
  2.7 1.6 %copy.5 = s32[128,3,512]{2,1,0:T(4,128)} copy(s32[128,3,512]{2,0,1:T(8,128)S(1)} %copy-done) | data formatting | bytes 1572864 | tf_op args[1]
  4.3 29.0 %shard_map.37 = f32[16,128]{1,0:T(8,128)} custom-call(f32[8,16,3,512]{3,2,1,0:T(4,128)} %bitcast.2, s32[8,16,3,512]{3,2,1,0:T(4,128)} %bitcast.3, f32[3]{0:T(128)} %box.1), custom_call_target="tpu_custom_call" | custom-call | tf_op jit(solution)/shard_map/pallas_call | solution.py:214
  33.3 1.3 %copy.7 = f32[16,128]{1,0:T(8,128)} copy(f32[16,128]{1,0:T(8,128)} %shard_map.37) | data formatting | bytes 16384
Async XLA Ops:
  0.0 2.7 %copy-start = (s32[128,3,512]{2,0,1:T(8,128)S(1)}, s32[128,3,512]{2,0,1:T(8,128)}, u32[]{:S(2)}) copy-start(s32[128,3,512]{2,0,1:T(8,128)} %param.4) | copy-start | bytes 2359300
where the time goes:
time: 34.9 us; the launch traced here: 34.6 us
  Pallas kernels  29 us (83%)
  local copies, waits for them, and re-layouts  5.6 us (16%)
    pallas_call x1, Pallas kernels, on_device(): pl.pallas_call(functools.partial(kernel, n), out_shape=jax.ShapeDtypeStru...  29 us
    unnamed x5, local copies, waits for them, and re-layouts  5.6 us

commit v1 on v0

--- a/solution.py
+++ b/solution.py
@@ -15,9 +15,8 @@
 
 def kernel(n, wrapped, crossings, box, out, wbuf, xbuf, sbuf, hbuf, mean_buf, delta_buf,
            ext, sq, lagbuf, tbuf, rbuf, load_sem, halo_send, halo_recv, part_send, part_recv):
-    dims, depth = wbuf.shape[0], wbuf.shape[1]
-    frames = SUB * depth
-    groups = sbuf.shape[0]
+    dims, groups, frames = wbuf.shape[:3]
+    depth = frames // SUB
     per_owner = out.shape[0]
     owners = LANES // per_owner
     me = lax.axis_index("tm")
@@ -26,11 +25,12 @@
     nxt = lax.rem(me + 1, n)
 
     def load(i, which):
-        c, s = i // SUB, lax.rem(i, SUB)
+        c, g = i // groups, lax.rem(i, groups)
+        lanes = pl.ds(pl.multiple_of(g * LANES, LANES), LANES)
         src, dst = ((wrapped, wbuf), (crossings, xbuf))[which]
-        return pltpu.make_async_copy(src.at[s, :, c, :], dst.at[c, :, s, :], load_sem.at[which, i])
-
-    @pl.loop(0, dims * SUB)
+        return pltpu.make_async_copy(src.at[c, :, lanes], dst.at[c, g], load_sem.at[which, i])
+
+    @pl.loop(0, dims * groups)
     def _(i):
         load(i, 0).start()
         load(i, 1).start()
@@ -41,7 +41,7 @@
     def _(o):
         pl.semaphore_signal(barrier, inc=1, device_id=(lax.rem(me + o, n),), device_id_type=MESH)
 
-    @pl.loop(0, dims * SUB)
+    @pl.loop(0, dims * groups)
     def _(i):
         load(i, 0).wait()
         load(i, 1).wait()
@@ -61,11 +61,10 @@
     def prepare(step):
         g = lax.rem(step // dims + first_group(prev), groups)
         c = lax.rem(step, dims)
-        lanes = pl.ds(pl.multiple_of(g * LANES, LANES), LANES)
         box_len = box[c]
-        counts = [xbuf[c, 0, :, lanes].astype(jnp.float32)]
+        counts = [xbuf[c, g, pl.ds(0, SUB, stride=depth), :].astype(jnp.float32)]
         for r in range(1, depth):
-            counts.append(counts[-1] + xbuf[c, r, :, lanes].astype(jnp.float32))
+            counts.append(counts[-1] + xbuf[c, g, pl.ds(r, SUB, stride=depth), :].astype(jnp.float32))
         incl = counts[-1]
         for shift in (1, 2, 4):
             incl = incl + jnp.where(sub_ids >= shift, pltpu.roll(incl, shift, 0), 0.0)
@@ -73,7 +72,7 @@
         before = incl - counts[-1]
         tot_pos = jnp.zeros((SUB, LANES), jnp.float32)
         for r in range(depth):
-            pos = (wbuf[c, r, :, lanes] + (counts[r] + before)) * box_len
+            pos = (wbuf[c, g, pl.ds(r, SUB, stride=depth), :] + (counts[r] + before)) * box_len
             sbuf[g, c, r] = pos
             tot_pos = tot_pos + pos
         mean = jnp.broadcast_to(jnp.sum(tot_pos, axis=0, keepdims=True), (SUB, LANES)) * (1.0 / frames)
@@ -193,9 +192,6 @@
             device_id=(src,), device_id_type=MESH).wait()
         out[...] = out[...] + rbuf[src]
 
-    lag_ids = lax.broadcasted_iota(jnp.int32, (per_owner, LAGS), 1)
-    out[...] = out[...] / (n * frames - lag_ids).astype(jnp.float32)
-
     @pl.when(me > 0)
     def _():
         @pl.loop(0, groups * dims)
@@ -208,17 +204,16 @@
     depth, groups = frames // SUB, atoms // LANES
     per_owner = atoms // n
     assert frames == LAGS and atoms % LANES == 0 and LANES % per_owner == 0
-    split = (SUB, depth, dims, atoms)
     any_spec = pl.BlockSpec(memory_space=pl.ANY)
     f32 = jnp.float32
-    return pl.pallas_call(
+    lag_sum = pl.pallas_call(
         functools.partial(kernel, n),
         out_shape=jax.ShapeDtypeStruct((per_owner, LAGS), f32),
         in_specs=[any_spec, any_spec, pl.BlockSpec(memory_space=pltpu.SMEM)],
         out_specs=pl.BlockSpec(memory_space=pltpu.VMEM),
         scratch_shapes=[
-            pltpu.VMEM((dims, depth, SUB, atoms), f32),
-            pltpu.VMEM((dims, depth, SUB, atoms), jnp.int32),
+            pltpu.VMEM((dims, groups, frames, LANES), f32),
+            pltpu.VMEM((dims, groups, frames, LANES), jnp.int32),
             pltpu.VMEM((groups, dims, depth, SUB, LANES), f32),
             pltpu.VMEM((groups, dims, depth, SUB, LANES), f32),
             pltpu.VMEM((groups, dims, SUB, LANES), f32),
@@ -228,14 +223,16 @@
             pltpu.VMEM((LAGS * SUB, LANES), f32),
             pltpu.VMEM((n, per_owner, LAGS), f32),
             pltpu.VMEM((n, per_owner, LAGS), f32),
-            pltpu.SemaphoreType.DMA((2, dims * SUB)),
+            pltpu.SemaphoreType.DMA((2, dims * groups)),
             pltpu.SemaphoreType.DMA((groups * dims,)),
             pltpu.SemaphoreType.DMA((groups * dims,)),
             pltpu.SemaphoreType.DMA((n,)),
             pltpu.SemaphoreType.DMA((n,)),
         ],
         compiler_params=pltpu.CompilerParams(collective_id=0, has_side_effects=True),
-    )(wrapped.reshape(split), crossings.reshape(split), box_size)
+    )(jnp.transpose(wrapped, (1, 0, 2)), jnp.transpose(crossings, (1, 0, 2)), box_size)
+    divisor = (n * frames - jnp.arange(LAGS, dtype=jnp.int32)).astype(f32)
+    return lag_sum / divisor[None, :]
 
 
 def solution(mesh):

time: 34.9 us -> 29.7 us (0.85)
  local copies, waits for them, and re-layouts: 5.6 us -> 0 us
  other arithmetic: 0 us -> 1.31 us
  Pallas kernels: 29 us -> 28.2 us
    unnamed x5 -> x0, local copies, waits for them, and re-layouts: 5.6 us -> none
    div x0 -> x1, other arithmetic: none -> 1.3 us  [on_device(): return lag_sum / divisor[None, :]]
    pallas_call x1, Pallas kernels: 29 us -> 28.2 us  [on_device(): pl.pallas_call(functools.partial(kernel, n), out_shape=jax.ShapeDtypeStru...]
where the time goes in v1:
time: 29.7 us; the launch traced here: 29.5 us
  Pallas kernels  28.2 us (95%)
  other arithmetic  1.31 us (4%)
    pallas_call x1, Pallas kernels, on_device(): pl.pallas_call(functools.partial(kernel, n), out_shape=jax.ShapeDtypeStru...  28.2 us
    div x1, other arithmetic, on_device(): return lag_sum / divisor[None, :]  1.3 us

profile of v1, /device:TPU:0, one launch (start us, length us, event | category | flops | bytes accessed | tf_op | source)
XLA Modules:
  0.0 29.5 jit_solution(11655273887999349786)
XLA Ops:
  0.0 28.2 %shard_map.37 = f32[16,128]{1,0:T(8,128)} custom-call(f32[3,128,512]{2,1,0:T(8,128)} %bitcast.2, s32[3,128,512]{2,1,0:T(8,128)} %bitcast.3, f32[3]{0:T(128)} %box.1), custom_call_target="tpu_custom_call" | custom-call | tf_op jit(solution)/shard_map/pallas_call | solution.py:209
  28.2 1.3 %broadcast_divide_fusion = f32[16,128]{1,0:T(8,128)} fusion(f32[16,128]{1,0:T(8,128)} %shard_map.37, f32[128]{0:T(128)S(1)} %subtract_convert_fusion), kind=kLoop, calls=%fused_computation | loop fusion | flops 2048 | bytes 16896 | tf_op jit(solution)/shard_map/div | solution.py:235
  (1 shorter events, 0.0 us)

commit v2 on v1

--- a/solution.py
+++ b/solution.py
@@ -10,11 +10,12 @@
 LAGS = 128
 LANES = 128
 SUB = 8
+TURNS = SUB // 2 + 1
 MESH = pl.DeviceIdType.MESH
 
 
 def kernel(n, wrapped, crossings, box, out, wbuf, xbuf, sbuf, hbuf, mean_buf, delta_buf,
-           ext, sq, lagbuf, tbuf, rbuf, load_sem, halo_send, halo_recv, part_send, part_recv):
+           own_ext, far_ext, inner_lag, cross_lag, sq, lagbuf, tbuf, rbuf, load_sem, halo_send, halo_recv, part_send, part_recv):
     dims, groups, frames = wbuf.shape[:3]
     depth = frames // SUB
     per_owner = out.shape[0]
@@ -40,6 +41,20 @@
     @pl.loop(1, n)
     def _(o):
         pl.semaphore_signal(barrier, inc=1, device_id=(lax.rem(me + o, n),), device_id_type=MESH)
+
+    zero = jnp.zeros((SUB, LANES), jnp.float32)
+
+    @pl.loop(0, groups * TURNS)
+    def _(i):
+        for d in range(2 * depth):
+            inner_lag[i, d] = zero
+            cross_lag[i, d] = zero
+
+    @pl.loop(0, groups)
+    def _(g):
+        for r in range(depth):
+            sq[g, r, 0:SUB, :] = zero
+            sq[g, r, SUB:2 * SUB, :] = zero
 
     @pl.loop(0, dims * groups)
     def _(i):
@@ -80,15 +95,76 @@
         delta_buf[g, c] = total * box_len - mean
         return g * dims + c
 
-    pl.semaphore_wait(barrier, n - 1)
+    def correlate(near, far, buf, row, offsets):
+        acc = {}
+        for m in range(depth):
+            moved = far(m)
+            for r in range(depth):
+                d = m - r
+                if d in offsets:
+                    term = moved * near[r]
+                    acc[d] = acc[d] + term if d in acc else term
+                    if m == depth - 1 or r == depth - 1:
+                        buf[row, d + depth - 1] = buf[row, d + depth - 1] + acc[d]
+
+    everything = range(1 - depth, depth)
+
+    def inner(step):
+        g = lax.rem(step // dims + first_group(me), groups)
+        c = lax.rem(step, dims)
+        mean = mean_buf[g, c]
+        for r in range(depth):
+            own = sbuf[g, c, r] - mean
+            own_ext[g, c, r, 0:SUB, :] = own
+            own_ext[g, c, r, SUB:2 * SUB, :] = own
+            sq[g, r, 0:SUB, :] = sq[g, r, 0:SUB, :] + own * own
+        near = [own_ext[g, c, r, 0:SUB, :] * -2.0 for r in range(depth)]
+        correlate(near, lambda m: own_ext[g, c, m, 0:SUB, :], inner_lag, g * TURNS, range(depth))
+
+        @pl.loop(1, TURNS)
+        def _(q):
+            near = [own_ext[g, c, r, 0:SUB, :] * -2.0 for r in range(depth)]
+            correlate(near, lambda m: own_ext[g, c, m, pl.ds(q, SUB), :], inner_lag, g * TURNS + q, everything)
+
+    def cross(g, c):
+        delta = delta_buf[g, c]
+        for r in range(depth):
+            far = hbuf[g, c, r] + delta
+            far_ext[r, 0:SUB, :] = far
+            far_ext[r, SUB:2 * SUB, :] = far
+            sq[g, r, SUB:2 * SUB, :] = sq[g, r, SUB:2 * SUB, :] + far * far
+        near = [own_ext[g, c, r, 0:SUB, :] * -2.0 for r in range(depth)]
+        correlate(near, lambda m: far_ext[m, 0:SUB, :], cross_lag, g * TURNS, range(1 - depth, 0))
+
+        @pl.loop(1, TURNS)
+        def _(q):
+            low = sub_ids < SUB - q
+            near = [jnp.where(low, own_ext[g, c, r, pl.ds(q, SUB), :], own_ext[g, c, r, 0:SUB, :]) * -2.0
+                    for r in range(depth)]
+            correlate(near, lambda m: jnp.where(low, far_ext[m, 0:SUB, :], far_ext[m, pl.ds(q, SUB), :]),
+                      cross_lag, g * TURNS + q, everything)
 
     @pl.loop(0, groups * dims)
     def _(step):
-        i = prepare(step)
-
-        @pl.when(me > 0)
-        def _():
-            halo(i).start()
+        prepare(step)
+
+    ahead = groups * dims // 2
+
+    @pl.loop(0, ahead)
+    def _(step):
+        inner(step)
+
+    pl.semaphore_wait(barrier, n - 1)
+
+    @pl.when(me > 0)
+    def _():
+        @pl.loop(0, groups * dims)
+        def _(step):
+            halo(lax.rem(step // dims + first_group(prev), groups) * dims + lax.rem(step, dims)).start()
+
+    @pl.loop(ahead, groups * dims)
+    def _(step):
+        inner(step)
 
     end_row = jnp.where(is_last, SUB, 4 * SUB)
 
@@ -103,65 +179,57 @@
     def _(gi):
         g = lax.rem(gi + first_group(me), groups)
 
-        @pl.loop(0, LAGS)
-        def _(k):
-            lagbuf[pl.ds(pl.multiple_of(k * SUB, SUB), SUB), :] = jnp.zeros((SUB, LANES), jnp.float32)
-
-        sq[...] = jnp.zeros_like(sq)
-
-        @pl.loop(0, dims)
-        def _(c):
-            mean, delta = mean_buf[g, c], delta_buf[g, c]
-            for r in range(depth):
-                own = sbuf[g, c, r] - mean
-                ext[r, 0:SUB, :] = own
-                sq[r, 0:SUB, :] = sq[r, 0:SUB, :] + own * own
-
-            @pl.when(is_last)
-            def _():
-                for r in range(depth):
-                    ext[r, SUB:2 * SUB, :] = jnp.zeros((SUB, LANES), jnp.float32)
-
-            @pl.when(jnp.logical_not(is_last))
-            def _():
+        @pl.when(jnp.logical_not(is_last))
+        def _():
+            @pl.loop(0, dims)
+            def _(c):
                 halo(g * dims + c).wait_recv()
-                for r in range(depth):
-                    far = hbuf[g, c, r] + delta
-                    ext[r, SUB:2 * SUB, :] = far
-                    sq[r, SUB:2 * SUB, :] = sq[r, SUB:2 * SUB, :] + far * far
-
-            @pl.loop(0, LAGS // depth)
-            def _(q):
-                near = [ext[r, 0:SUB, :] * -2.0 for r in range(depth)]
-                rows = [pl.ds(pl.multiple_of((q * depth + j) * SUB, SUB), SUB) for j in range(depth)]
-                acc = [None] * depth
-                for m in range(2 * depth - 1):
-                    far = ext[m % depth, pl.ds(q + m // depth, SUB), :]
-                    for r in range(max(0, m - depth + 1), min(depth - 1, m) + 1):
-                        j = m - r
-                        term = far * near[r]
-                        acc[j] = term if acc[j] is None else acc[j] + term
-                        if r == depth - 1:
-                            lagbuf[rows[j], :] = lagbuf[rows[j], :] + acc[j]
-
-        own_total = sq[0, 0:SUB, :]
+                cross(g, c)
+
+        def ins(q, d):
+            return inner_lag[g * TURNS + q, d + depth - 1]
+
+        def crs(q, d):
+            return cross_lag[g * TURNS + q, d + depth - 1]
+
+        half = SUB // 2
+        lows = [sub_ids < SUB - q for q in range(TURNS)]
+        for k in range(LAGS):
+            q, j = k // depth, k % depth
+            if q == 0:
+                val = ins(0, j)
+            elif q <= half:
+                val = jnp.where(lows[q], ins(q, j), crs(q, j))
+            else:
+                val = jnp.where(lows[SUB - q], crs(SUB - q, j), ins(SUB - q, -j))
+            if j > 0:
+                if q < half:
+                    val = val + jnp.where(lows[q + 1], ins(q + 1, j - depth), crs(q + 1, j - depth))
+                elif q < SUB - 1:
+                    p = SUB - 1 - q
+                    val = val + jnp.where(lows[p], crs(p, j - depth), ins(p, depth - j))
+                else:
+                    val = val + crs(0, j - depth)
+            lagbuf[k * SUB:(k + 1) * SUB, :] = val
+
+        own_total = sq[g, 0, 0:SUB, :]
         for r in range(1, depth):
-            own_total = own_total + sq[r, 0:SUB, :]
+            own_total = own_total + sq[g, r, 0:SUB, :]
 
         @pl.loop(0, LAGS // depth)
         def _(q):
             row = sub_ids + q
             near_sum = own_total
-            far_sum = sq[0, pl.ds(q, SUB), :]
+            far_sum = sq[g, 0, pl.ds(q, SUB), :]
             for r in range(1, depth):
-                far_sum = far_sum + sq[r, pl.ds(q, SUB), :]
+                far_sum = far_sum + sq[g, r, pl.ds(q, SUB), :]
             for j in range(depth):
                 base = jnp.where(row >= end_row, 0.0, jnp.where(row == end_row - 1, near_sum, own_total))
                 rows = pl.ds(pl.multiple_of((q * depth + j) * SUB, SUB), SUB)
                 lagbuf[rows, :] = lagbuf[rows, :] + (base + far_sum)
                 if j < depth - 1:
-                    near_sum = near_sum - sq[depth - 1 - j, 0:SUB, :]
-                    far_sum = far_sum + (sq[j, pl.ds(q + 1, SUB), :] - sq[j, pl.ds(q, SUB), :])
+                    near_sum = near_sum - sq[g, depth - 1 - j, 0:SUB, :]
+                    far_sum = far_sum + (sq[g, j, pl.ds(q + 1, SUB), :] - sq[g, j, pl.ds(q, SUB), :])
 
         blocks = []
         for kb in range(LAGS // SUB):
@@ -218,8 +286,11 @@
             pltpu.VMEM((groups, dims, depth, SUB, LANES), f32),
             pltpu.VMEM((groups, dims, SUB, LANES), f32),
             pltpu.VMEM((groups, dims, SUB, LANES), f32),
+            pltpu.VMEM((groups, dims, depth, 2 * SUB, LANES), f32),
             pltpu.VMEM((depth, 2 * SUB, LANES), f32),
-            pltpu.VMEM((depth, 2 * SUB, LANES), f32),
+            pltpu.VMEM((groups * TURNS, 2 * depth, SUB, LANES), f32),
+            pltpu.VMEM((groups * TURNS, 2 * depth, SUB, LANES), f32),
+            pltpu.VMEM((groups, depth, 2 * SUB, LANES), f32),
             pltpu.VMEM((LAGS * SUB, LANES), f32),
             pltpu.VMEM((n, per_owner, LAGS), f32),
             pltpu.VMEM((n, per_owner, LAGS), f32),

time: 29.7 us -> 27.5 us (0.926)
  Pallas kernels: 28.2 us -> 25.9 us
    pallas_call x1, Pallas kernels: 28.2 us -> 25.9 us  [on_device(): pl.pallas_call(functools.partial(kernel, n), out_shape=jax.ShapeDtypeStru...]
where the time goes in v2:
time: 27.5 us; the launch traced here: 27.2 us
  Pallas kernels  25.9 us (94%)
  other arithmetic  1.31 us (5%)
    pallas_call x1, Pallas kernels, on_device(): pl.pallas_call(functools.partial(kernel, n), out_shape=jax.ShapeDtypeStru...  25.9 us
    div x1, other arithmetic, on_device(): return lag_sum / divisor[None, :]  1.3 us

profile of v2, /device:TPU:0, one launch (start us, length us, event | category | flops | bytes accessed | tf_op | source)
XLA Modules:
  0.0 27.2 jit_solution(10920323648809305117)
XLA Ops:
  0.0 25.9 %shard_map.37 = f32[16,128]{1,0:T(8,128)} custom-call(f32[3,128,512]{2,1,0:T(8,128)} %bitcast.2, s32[3,128,512]{2,1,0:T(8,128)} %bitcast.3, f32[3]{0:T(128)} %box.1), custom_call_target="tpu_custom_call" | custom-call | tf_op jit(solution)/shard_map/pallas_call | solution.py:277
  25.9 1.3 %broadcast_divide_fusion = f32[16,128]{1,0:T(8,128)} fusion(f32[16,128]{1,0:T(8,128)} %shard_map.37, f32[128]{0:T(128)S(1)} %subtract_convert_fusion), kind=kLoop, calls=%fused_computation | loop fusion | flops 2048 | bytes 16896 | tf_op jit(solution)/shard_map/div | solution.py:306
  (1 shorter events, 0.0 us)

commit v3 on v2

--- a/solution.py
+++ b/solution.py
@@ -25,22 +25,22 @@
     prev = lax.rem(me + n - 1, n)
     nxt = lax.rem(me + 1, n)
 
+    barrier = pltpu.get_barrier_semaphore()
+
+    @pl.loop(1, n)
+    def _(o):
+        pl.semaphore_signal(barrier, inc=1, device_id=(lax.rem(me + o, n),), device_id_type=MESH)
+
     def load(i, which):
         c, g = i // groups, lax.rem(i, groups)
         lanes = pl.ds(pl.multiple_of(g * LANES, LANES), LANES)
         src, dst = ((wrapped, wbuf), (crossings, xbuf))[which]
-        return pltpu.make_async_copy(src.at[c, :, lanes], dst.at[c, g], load_sem.at[which, i])
+        return pltpu.make_async_copy(src.at[c, :, lanes], dst.at[c, g], load_sem.at[which])
 
     @pl.loop(0, dims * groups)
     def _(i):
         load(i, 0).start()
         load(i, 1).start()
-
-    barrier = pltpu.get_barrier_semaphore()
-
-    @pl.loop(1, n)
-    def _(o):
-        pl.semaphore_signal(barrier, inc=1, device_id=(lax.rem(me + o, n),), device_id_type=MESH)
 
     zero = jnp.zeros((SUB, LANES), jnp.float32)
 
@@ -56,10 +56,8 @@
             sq[g, r, 0:SUB, :] = zero
             sq[g, r, SUB:2 * SUB, :] = zero
 
-    @pl.loop(0, dims * groups)
-    def _(i):
-        load(i, 0).wait()
-        load(i, 1).wait()
+    pltpu.make_async_copy(wbuf, wbuf, load_sem.at[0]).wait()
+    pltpu.make_async_copy(xbuf, xbuf, load_sem.at[1]).wait()
 
     sub_ids = lax.broadcasted_iota(jnp.int32, (SUB, LANES), 0)
 
@@ -67,7 +65,7 @@
         return pltpu.make_async_remote_copy(
             src_ref=sbuf.at[i // dims, lax.rem(i, dims)],
             dst_ref=hbuf.at[i // dims, lax.rem(i, dims)],
-            send_sem=halo_send.at[i], recv_sem=halo_recv.at[i],
+            send_sem=halo_send, recv_sem=halo_recv.at[i],
             device_id=(prev,), device_id_type=MESH)
 
     def first_group(device):
@@ -148,7 +146,7 @@
     def _(step):
         prepare(step)
 
-    ahead = groups * dims // 2
+    ahead = groups * dims // 3
 
     @pl.loop(0, ahead)
     def _(step):
@@ -172,7 +170,7 @@
         owner = g * owners + d
         return owner, pltpu.make_async_remote_copy(
             src_ref=tbuf.at[owner], dst_ref=rbuf.at[me],
-            send_sem=part_send.at[owner], recv_sem=part_recv.at[me],
+            send_sem=part_send, recv_sem=part_recv,
             device_id=(owner,), device_id_type=MESH)
 
     @pl.loop(0, groups)
@@ -249,22 +247,18 @@
             def _():
                 copy.start()
 
-    out[...] = tbuf[me]
-
-    @pl.loop(1, n)
-    def _(o):
-        src = lax.rem(me + o, n)
-        pltpu.make_async_remote_copy(
-            src_ref=tbuf.at[src], dst_ref=rbuf.at[src],
-            send_sem=part_send.at[src], recv_sem=part_recv.at[src],
-            device_id=(src,), device_id_type=MESH).wait()
-        out[...] = out[...] + rbuf[src]
+    rbuf[me] = tbuf[me]
+    others = pl.ds(0, n - 1)
+    pltpu.make_async_remote_copy(
+        src_ref=tbuf.at[others], dst_ref=rbuf.at[others], send_sem=part_send, recv_sem=part_recv,
+        device_id=(nxt,), device_id_type=MESH).wait()
+    out[...] = jnp.sum(rbuf[...], axis=0)
 
     @pl.when(me > 0)
     def _():
-        @pl.loop(0, groups * dims)
-        def _(i):
-            halo(i).wait_send()
+        pltpu.make_async_remote_copy(
+            src_ref=sbuf, dst_ref=hbuf, send_sem=halo_send, recv_sem=halo_recv.at[0],
+            device_id=(prev,), device_id_type=MESH).wait_send()
 
 
 def on_device(n, wrapped, crossings, box_size):
@@ -294,11 +288,11 @@
             pltpu.VMEM((LAGS * SUB, LANES), f32),
             pltpu.VMEM((n, per_owner, LAGS), f32),
             pltpu.VMEM((n, per_owner, LAGS), f32),
-            pltpu.SemaphoreType.DMA((2, dims * groups)),
+            pltpu.SemaphoreType.DMA((2,)),
+            pltpu.SemaphoreType.DMA,
             pltpu.SemaphoreType.DMA((groups * dims,)),
-            pltpu.SemaphoreType.DMA((groups * dims,)),
-            pltpu.SemaphoreType.DMA((n,)),
-            pltpu.SemaphoreType.DMA((n,)),
+            pltpu.SemaphoreType.DMA,
+            pltpu.SemaphoreType.DMA,
         ],
         compiler_params=pltpu.CompilerParams(collective_id=0, has_side_effects=True),
     )(jnp.transpose(wrapped, (1, 0, 2)), jnp.transpose(crossings, (1, 0, 2)), box_size)

time: 27.5 us -> 26.3 us (0.956)
  Pallas kernels: 25.9 us -> 24.8 us
    pallas_call x1, Pallas kernels: 25.9 us -> 24.8 us  [on_device(): pl.pallas_call(functools.partial(kernel, n), out_shape=jax.ShapeDtypeStru...]
where the time goes in v3:
time: 26.3 us; the launch traced here: 26.1 us
  Pallas kernels  24.8 us (94%)
  other arithmetic  1.31 us (5%)
    pallas_call x1, Pallas kernels, on_device(): pl.pallas_call(functools.partial(kernel, n), out_shape=jax.ShapeDtypeStru...  24.8 us
    div x1, other arithmetic, on_device(): return lag_sum / divisor[None, :]  1.3 us

profile of v3, /device:TPU:0, one launch (start us, length us, event | category | flops | bytes accessed | tf_op | source)
XLA Modules:
  0.0 26.1 jit_solution(12395110985558402134)
XLA Ops:
  0.0 24.8 %shard_map.37 = f32[16,128]{1,0:T(8,128)} custom-call(f32[3,128,512]{2,1,0:T(8,128)} %bitcast.2, s32[3,128,512]{2,1,0:T(8,128)} %bitcast.3, f32[3]{0:T(128)} %box.1), custom_call_target="tpu_custom_call" | custom-call | tf_op jit(solution)/shard_map/pallas_call | solution.py:271
  24.8 1.3 %broadcast_divide_fusion = f32[16,128]{1,0:T(8,128)} fusion(f32[16,128]{1,0:T(8,128)} %shard_map.37, f32[128]{0:T(128)S(1)} %subtract_convert_fusion), kind=kLoop, calls=%fused_computation | loop fusion | flops 2048 | bytes 16896 | tf_op jit(solution)/shard_map/div | solution.py:300
  (1 shorter events, 0.0 us)

commit v4 on v3

--- a/solution.py
+++ b/solution.py
@@ -29,7 +29,7 @@
 
     @pl.loop(1, n)
     def _(o):
-        pl.semaphore_signal(barrier, inc=1, device_id=(lax.rem(me + o, n),), device_id_type=MESH)
+        pl.semaphore_signal(barrier, inc=1, device_id=(lax.rem(me + n - o, n),), device_id_type=MESH)
 
     def load(i, which):
         c, g = i // groups, lax.rem(i, groups)
@@ -190,6 +190,10 @@
         def crs(q, d):
             return cross_lag[g * TURNS + q, d + depth - 1]
 
+        own_total = sq[g, 0, 0:SUB, :]
+        for r in range(1, depth):
+            own_total = own_total + sq[g, r, 0:SUB, :]
+
         half = SUB // 2
         lows = [sub_ids < SUB - q for q in range(TURNS)]
         for k in range(LAGS):
@@ -208,26 +212,17 @@
                     val = val + jnp.where(lows[p], crs(p, j - depth), ins(p, depth - j))
                 else:
                     val = val + crs(0, j - depth)
-            lagbuf[k * SUB:(k + 1) * SUB, :] = val
-
-        own_total = sq[g, 0, 0:SUB, :]
-        for r in range(1, depth):
-            own_total = own_total + sq[g, r, 0:SUB, :]
-
-        @pl.loop(0, LAGS // depth)
-        def _(q):
-            row = sub_ids + q
-            near_sum = own_total
-            far_sum = sq[g, 0, pl.ds(q, SUB), :]
-            for r in range(1, depth):
-                far_sum = far_sum + sq[g, r, pl.ds(q, SUB), :]
-            for j in range(depth):
-                base = jnp.where(row >= end_row, 0.0, jnp.where(row == end_row - 1, near_sum, own_total))
-                rows = pl.ds(pl.multiple_of((q * depth + j) * SUB, SUB), SUB)
-                lagbuf[rows, :] = lagbuf[rows, :] + (base + far_sum)
-                if j < depth - 1:
-                    near_sum = near_sum - sq[g, depth - 1 - j, 0:SUB, :]
-                    far_sum = far_sum + (sq[g, j, pl.ds(q + 1, SUB), :] - sq[g, j, pl.ds(q, SUB), :])
+            if j == 0:
+                row = sub_ids + q
+                near_sum = own_total
+                far_sum = sq[g, 0, q:q + SUB, :]
+                for r in range(1, depth):
+                    far_sum = far_sum + sq[g, r, q:q + SUB, :]
+            else:
+                near_sum = near_sum - sq[g, depth - j, 0:SUB, :]
+                far_sum = far_sum + (sq[g, j - 1, q + 1:q + 1 + SUB, :] - sq[g, j - 1, q:q + SUB, :])
+            base = jnp.where(row >= end_row, 0.0, jnp.where(row == end_row - 1, near_sum, own_total))
+            lagbuf[k * SUB:(k + 1) * SUB, :] = val + (base + far_sum)
 
         blocks = []
         for kb in range(LAGS // SUB):

time: 26.3 us -> 26.4 us (level)
  no operation moved by 1% of the time
where the time goes in v4:
time: 26.4 us; the launch traced here: 26.1 us
  Pallas kernels  24.8 us (94%)
  other arithmetic  1.31 us (5%)
    pallas_call x1, Pallas kernels, on_device(): pl.pallas_call(functools.partial(kernel, n), out_shape=jax.ShapeDtypeStru...  24.8 us
    div x1, other arithmetic, on_device(): return lag_sum / divisor[None, :]  1.3 us

profile of v4, /device:TPU:0, one launch (start us, length us, event | category | flops | bytes accessed | tf_op | source)
XLA Modules:
  0.0 26.1 jit_solution(2706709633063942913)
XLA Ops:
  0.0 24.8 %shard_map.37 = f32[16,128]{1,0:T(8,128)} custom-call(f32[3,128,512]{2,1,0:T(8,128)} %bitcast.2, s32[3,128,512]{2,1,0:T(8,128)} %bitcast.3, f32[3]{0:T(128)} %box.1), custom_call_target="tpu_custom_call" | custom-call | tf_op jit(solution)/shard_map/pallas_call | solution.py:266
  24.8 1.3 %broadcast_divide_fusion = f32[16,128]{1,0:T(8,128)} fusion(f32[16,128]{1,0:T(8,128)} %shard_map.37, f32[128]{0:T(128)S(1)} %subtract_convert_fusion), kind=kLoop, calls=%fused_computation | loop fusion | flops 2048 | bytes 16896 | tf_op jit(solution)/shard_map/div | solution.py:295
  (1 shorter events, 0.0 us)
